TPU v7x, 32 devices: a whole 2x2x4 slice. The times are simulated.
32 devices in a mesh: row: 4 (over y, x), col: 4 (over z), depth: 2 (over core).
Axes of the slice: x: 2, y: 2, z: 4, core: 2. Of those that a mesh axis runs over, the one named last changes fastest.
Arguments:
- matrix_panel: bfloat16 [12288, 65536], P('row', 'col'), may hold values from -0.1484375 to 0.1484375
- start_block: bfloat16 [12288, 64], P('row', 'depth'), may hold values from -6 to 6
- stored_basis: float32 [12288, 1024], P('row'), may hold values from -2.2 to 2.2
Outputs:
- new_block: float32 [12288, 64], P('row', 'depth')
- coefficients: float32 [1024, 64], P(None, 'depth')
- triangle: float32 [64, 64], replicated
All inputs are finite; a program needn't handle non-finite values.
Results may differ from a plain program's by a relative error of at most 0.0023.
Values may be sent and summed in bfloat16 or wider, within the bound.
A program may use at most 256 MiB of HBM per device.

v0:
```python
import jax
import jax.numpy as jnp
from jax import lax
from jax.sharding import PartitionSpec as P

HIGHEST = lax.Precision.HIGHEST


def contract_rows(left_side, right_side, mode):
    return lax.dot_general(
        left_side,
        right_side,
        (((0,), (0,)), ((), ())),
        precision=mode,
        preferred_element_type=jnp.float32,
    )


def factor_gram(gram_matrix):
    lower_factor = jnp.linalg.cholesky(gram_matrix)
    identity = jnp.eye(gram_matrix.shape[0], dtype=jnp.float32)
    inverse = jax.scipy.linalg.solve_triangular(lower_factor, identity, lower=True)
    return (lower_factor, inverse)


def orthonormal_pass(stored_basis, block_cols, reduce_sum, row_total):
    projection = reduce_sum(contract_rows(stored_basis, block_cols, HIGHEST)) / row_total
    remainder = block_cols - jnp.dot(
        stored_basis, projection, precision=HIGHEST, preferred_element_type=jnp.float32
    )
    gram_matrix = reduce_sum(contract_rows(remainder, remainder, HIGHEST)) / row_total
    lower_factor, inverse = factor_gram(gram_matrix)
    normed = jnp.dot(remainder, inverse.T, precision=HIGHEST, preferred_element_type=jnp.float32)
    return (projection, lower_factor, normed)


def per_device(matrix_panel, start_block, stored_basis):
    row_total = stored_basis.shape[0] * lax.axis_size("row")
    half_cols = start_block.shape[1]
    depth_index = lax.axis_index("depth")
    whole_start = lax.all_gather(start_block, "depth", axis=1, tiled=True)
    half_rows = matrix_panel.shape[0] // 2
    panel_rows = lax.dynamic_slice_in_dim(matrix_panel, depth_index * half_rows, half_rows, 0)
    start_rows = lax.dynamic_slice_in_dim(whole_start, depth_index * half_rows, half_rows, 0)
    basis_rows = lax.dynamic_slice_in_dim(stored_basis, depth_index * half_rows, half_rows, 0)
    mixed_cols = lax.psum(contract_rows(panel_rows, start_rows, None), ("row", "depth")).astype(
        jnp.bfloat16
    )
    image_block = lax.psum(
        jnp.dot(panel_rows, mixed_cols, preferred_element_type=jnp.float32), "col"
    )

    def sum_layers(value):
        return lax.psum(value, ("row", "depth"))

    proj_first, lower_first, normed_first = orthonormal_pass(
        basis_rows, image_block, sum_layers, row_total
    )
    proj_second, lower_second, normed_second = orthonormal_pass(
        basis_rows, normed_first, sum_layers, row_total
    )
    new_block = lax.all_to_all(normed_second, "depth", split_axis=1, concat_axis=0, tiled=True)
    coef_whole = proj_first + jnp.dot(
        proj_second, lower_first.T, precision=HIGHEST, preferred_element_type=jnp.float32
    )
    coefficients = lax.dynamic_slice_in_dim(coef_whole, depth_index * half_cols, half_cols, 1)
    triangle = jnp.dot(
        lower_second.T, lower_first.T, precision=HIGHEST, preferred_element_type=jnp.float32
    )
    return (new_block, coefficients, triangle)


def solution(mesh):
    placed = (P("row", "col"), P("row", "depth"), P("row", None))
    return jax.shard_map(
        per_device,
        mesh=mesh,
        in_specs=placed,
        out_specs=(P("row", "depth"), P(None, "depth"), P()),
        check_vma=False,
    )
```

profile of v0, /device:TPU:0, one launch (start us, length us, event | category | flops | bytes accessed | tf_op | source)
XLA Modules:
  0.0 405.6 jit_solution(3928022254567349980)
XLA Ops:
  7.2 0.0 all-reduce.5.cloned.1.call-start
  7.2 2.4 all_gather.3
  9.6 20.5 %fusion.2 = f32[16384,64]{0,1:T(8,128)} fusion(bf16[3072,16384]{1,0:T(8,128)(2,1)} %param.6, s32[]{:T(128)S(6)} %select_n.11, bf16[3072,64]{0,1:T(8,128)(2,1)S(1)} %all_gather.3), kind=kOutput, calls=%fused_computation.2 | convolution fusion | flops 3221225472 | bytes 54723584 | tf_op jit(solution)/shard_map/dot_general | solution.py:10
  30.1 89.5 %all-reduce.10 = bf16[16384,64]{0,1:T(8,128)(2,1)S(1)} all-reduce(f32[16384,64]{0,1:T(8,128)} %fusion.2), channel_id=1, replica_groups=mesh['row'=4,'col'=4,'depth'=2] {'row','depth'}, use_global_device_ids=true, to_apply=%region_0.0 | all-reduce | flops 1048576 | bytes 6291456 | tf_op jit(solution)/shard_map/psum | solution.py:46
  119.6 22.6 %fusion = f32[1536,64]{0,1:T(8,128)} fusion(bf16[3072,16384]{1,0:T(8,128)(2,1)} %param.6, s32[]{:T(128)S(6)} %select_n.11, bf16[16384,64]{0,1:T(8,128)(2,1)S(1)} %all-reduce.10), kind=kOutput, calls=%fused_computation | convolution fusion | flops 3221225472 | bytes 52822020 | tf_op jit(solution)/shard_map/dot_general | solution.py:50
  142.2 0.0 all-reduce.5.cloned.1.call-update
  142.2 0.0 all-reduce.7.cloned.1.call-start
  142.3 36.9 %all-reduce.5.cloned.1.call-done = f32[1536,64]{0,1:T(8,128)} async-done(((f32[1536,64]{0,1:T(8,128)}), f32[1536,64]{0,1:T(8,128)}) %all-reduce.5.cloned.1.call-update) | async-done | bytes 393232 | tf_op jit(solution)/shard_map/psum | solution.py:49
  179.2 7.6 %fusion.10 = f32[1024,64]{0,1:T(8,128)} fusion(f32[1536,64]{0,1:T(8,128)} %all-reduce.5.cloned.1.call-done, f32[3072,1024]{1,0:T(8,128)} %param.8, s32[]{:T(128)S(6)} %select_n.11), kind=kOutput, calls=%fused_computation.10 | convolution fusion | flops 1207959552 | bytes 6946820 | tf_op jit(solution)/shard_map/dot_general | solution.py:10
  186.8 0.0 all-reduce.7.cloned.1.call-update
  186.8 0.2 all-reduce.9.cloned.1.call-start
  187.0 53.1 %all-reduce.7.cloned.1.call-done = f32[1024,64]{0,1:T(8,128)} async-done(((f32[1024,64]{0,1:T(8,128)}), f32[1024,64]{0,1:T(8,128)}) %all-reduce.7.cloned.1.call-update) | async-done | bytes 262160 | tf_op jit(solution)/shard_map/psum | solution.py:54
  240.1 0.0 copy-start
  240.1 9.1 %fusion.12 = f32[1536,64]{0,1:T(8,128)S(1)} fusion(f32[1536,64]{0,1:T(8,128)} %all-reduce.5.cloned.1.call-done, f32[3072,1024]{1,0:T(8,128)} %param.8, s32[]{:T(128)S(6)} %select_n.11, f32[1024,64]{0,1:T(8,128)} %all-reduce.7.cloned.1.call-done), kind=kOutput, calls=%fused_computation.12 | convolution fusion | flops 1208123392 | bytes 7340036 | tf_op jit(solution)/shard_map/dot_general | solution.py:28
  249.2 0.5 fusion.56
  249.6 22.4 %psum.45 = f32[64,64]{0,1:T(8,128)S(1)} all-reduce(f32[64,64]{0,1:T(8,128)S(1)} %fusion.56), channel_id=1, replica_groups=mesh['row'=4,'col'=4,'depth'=2] {'row','depth'}, use_global_device_ids=true, to_apply=%region_3.0 | all-reduce | flops 4096 | bytes 32768 | tf_op jit(solution)/shard_map/psum | solution.py:54
  272.0 0.1 copy.12
  272.1 5.8 %cholesky.44 = f32[64,64]{1,0:T(8,128)S(1)} custom-call(f32[64,64]{1,0:T(8,128)S(1)} %fusion.32), custom_call_target="Cholesky" | custom-call | tf_op jit(solution)/shard_map/jit(cholesky)/cholesky | solution.py:20
  278.0 0.6 compare_reduce_fusion.1
  278.6 0.7 select_bitcast_fusion.1
  279.3 4.9 %custom-call.6 = f32[1,64,64]{1,2,0:T(8,128)S(1)} custom-call(f32[1,64,64]{2,1,0:T(8,128)S(1)} %select_bitcast_fusion.1), custom_call_target="InvertDiagBlocksLowerTriangular" | custom-call | tf_op jit(solution)/shard_map/jit(_solve_triangular)/triangular_solve | solution.py:22
  284.2 0.3 fusion.27
  284.4 0.5 fusion.57
  284.9 7.6 %fusion.6 = f32[1024,64]{0,1:T(8,128)} fusion(f32[1536,64]{0,1:T(8,128)S(1)} %fusion.57, f32[3072,1024]{1,0:T(8,128)} %param.8, s32[]{:T(128)S(6)} %select_n.11), kind=kOutput, calls=%fused_computation.6 | convolution fusion | flops 1207959552 | bytes 6946820 | tf_op jit(solution)/shard_map/dot_general | solution.py:10
  292.5 0.0 all-reduce.9.cloned.1.call-update
  292.5 0.0 copy-done
  292.5 53.0 %all-reduce.9.cloned.1.call-done = f32[1024,64]{0,1:T(8,128)} async-done(((f32[1024,64]{0,1:T(8,128)}), f32[1024,64]{0,1:T(8,128)}) %all-reduce.9.cloned.1.call-update) | async-done | bytes 262160 | tf_op jit(solution)/shard_map/psum | solution.py:54
  345.5 8.1 %fusion.15 = f32[1536,64]{0,1:T(8,128)S(1)} fusion(f32[1536,64]{0,1:T(8,128)S(1)} %fusion.57, f32[3072,1024]{1,0:T(8,128)} %param.8, s32[]{:T(128)S(6)} %select_n.11, f32[1024,64]{0,1:T(8,128)} %all-reduce.9.cloned.1.call-done), kind=kOutput, calls=%fused_computation.13 | convolution fusion | flops 1208123392 | bytes 7340036 | tf_op jit(solution)/shard_map/dot_general | solution.py:28
  353.7 0.5 fusion.58
  354.1 22.4 %psum.47 = f32[64,64]{0,1:T(8,128)S(1)} all-reduce(f32[64,64]{0,1:T(8,128)S(1)} %fusion.58), channel_id=1, replica_groups=mesh['row'=4,'col'=4,'depth'=2] {'row','depth'}, use_global_device_ids=true, to_apply=%region_7.10 | all-reduce | flops 4096 | bytes 32768 | tf_op jit(solution)/shard_map/psum | solution.py:54
  376.5 0.1 copy.14
  376.6 5.8 %cholesky.55 = f32[64,64]{1,0:T(8,128)S(1)} custom-call(f32[64,64]{1,0:T(8,128)S(1)} %fusion.30), custom_call_target="Cholesky" | custom-call | tf_op jit(solution)/shard_map/jit(cholesky)/cholesky | solution.py:20
  382.5 0.6 compare_reduce_fusion
  383.1 2.1 fusion.34
  385.3 0.7 select_bitcast_fusion
  385.9 4.9 %custom-call.7 = f32[1,64,64]{1,2,0:T(8,128)S(1)} custom-call(f32[1,64,64]{2,1,0:T(8,128)S(1)} %select_bitcast_fusion), custom_call_target="InvertDiagBlocksLowerTriangular" | custom-call | tf_op jit(solution)/shard_map/jit(_solve_triangular)/triangular_solve | solution.py:22
  390.8 0.3 fusion.25
  391.1 0.5 fusion.59
  391.6 4.0 all_to_all.19
  395.6 0.8 copy.18
  396.4 2.0 fusion.19
  398.4 0.7 dynamic-slice_add_fusion
  (7 shorter events, 0.1 us)
Async XLA Ops:
  7.2 172.0 %all-reduce.5.cloned.1.call-start = ((), (), s32[]{:S(2)}) async-start(), calls=%async_computation.1 | async-start | bytes 786432 | tf_op jit(solution)/shard_map/psum | solution.py:49
  142.2 97.8 %all-reduce.7.cloned.1.call-start = ((), (), s32[]{:S(2)}) async-start(), calls=%async_computation.2 | async-start | bytes 524288 | tf_op jit(solution)/shard_map/psum | solution.py:54
  186.8 158.8 %all-reduce.9.cloned.1.call-start = ((), (), s32[]{:S(2)}) async-start(), calls=%async_computation.3 | async-start | bytes 524288 | tf_op jit(solution)/shard_map/psum | solution.py:54
  240.1 52.4 %copy-start = (f32[1024,64]{0,1:T(8,128)S(1)}, f32[1024,64]{0,1:T(8,128)}, u32[]{:S(2)}) copy-start(f32[1024,64]{0,1:T(8,128)} %all-reduce.7.cloned.1.call-done) | copy-start | bytes 786436
Sparse Core Ops, SparseCore 0:
  142.3 36.8 all-reduce.4
  186.9 53.1 all-reduce.6
  292.6 52.8 all-reduce.8
where the time goes:
time: 406 us
  waiting for transfers between devices  143 us (35%)
  blocking collectives  141 us (35%)
  matrix products  82 us (20%)
  other arithmetic  24.9 us (6%)
  between operations  13.9 us (3%)
    psum x2, waiting for transfers between devices, sum_layers(): return lax.psum(value, ('row', 'depth'))  106 us
    psum x1, blocking collectives, per_device(): lax.psum(contract_rows(panel_rows, start_rows, None), ('row', 'depth'))  89.5 us
    psum x2, blocking collectives, sum_layers(): return lax.psum(value, ('row', 'depth'))  44.7 us
    psum x1, waiting for transfers between devices, per_device(): lax.psum(jnp.dot(panel_rows, mixed_cols, preferred_element_type=jnp.float...  36.9 us
    dot_general x5, matrix products, contract_rows(): lax.dot_general(left_side, right_side, (((0,), (0,)), ((), ())), precisio...  36.5 us
    dot_general x1, matrix products, per_device(): jnp.dot(panel_rows, mixed_cols, preferred_element_type=jnp.float32)  22.6 us
    dot_general x2, matrix products, orthonormal_pass(): jnp.dot(stored_basis, projection, precision=HIGHEST, preferred_element_ty...  17.2 us
    another operation x6, other arithmetic, factor_gram(): lower_factor = jnp.linalg.cholesky(gram_matrix)  13 us
  transfers between devices with their start and end apart: 3, of which 3 were waited for; matrix products, arithmetic and copies ran while one was open for 0% of the time, Pallas kernels for 0%

commit v1 on v0

--- a/solution.py
+++ b/solution.py
@@ -1,9 +1,19 @@
+import functools
 import jax
 import jax.numpy as jnp
 from jax import lax
 from jax.sharding import PartitionSpec as P
+from jax.lax import psum
 
 HIGHEST = lax.Precision.HIGHEST
+
+
+def find_zone_for(target, device_axis, mesh_ax):
+    r2 = psum(psum(target, device_axis), mesh_ax)
+    return r2
+
+
+terms_meet = functools.partial(find_zone_for, device_axis="depth", mesh_ax="row")
 
 
 def contract_rows(left_side, right_side, mode):
@@ -51,7 +61,7 @@
     )
 
     def sum_layers(value):
-        return lax.psum(value, ("row", "depth"))
+        return terms_meet(value)
 
     proj_first, lower_first, normed_first = orthonormal_pass(
         basis_rows, image_block, sum_layers, row_total

time: 406 us -> 423 us (1.042)
  waiting for transfers between devices: 143 us -> 167 us
  blocking collectives: 141 us -> 133 us
    psum x2 -> x4, waiting for transfers between devices: 106 us -> 130 us  [find_zone_for(): r2 = psum(psum(target, device_axis), mesh_ax)]
    psum x2 -> x4, blocking collectives: 44.7 us -> 37.5 us  [find_zone_for(): r2 = psum(psum(target, device_axis), mesh_ax)]
  transfers between devices with their start and end apart: 3 -> 5, of which waited for: 3 -> 5; matrix products, arithmetic and copies ran while one was open for 0% -> 0% of each run, Pallas kernels for 0% -> 0%
where the time goes in v1:
time: 423 us; the launch traced here: 422 us
  waiting for transfers between devices  167 us (39%)
  blocking collectives  133 us (31%)
  matrix products  82 us (19%)
  other arithmetic  24.9 us (6%)
  between operations  13.9 us (3%)
    psum x4, waiting for transfers between devices, find_zone_for(): r2 = psum(psum(target, device_axis), mesh_ax)  130 us
    psum x1, blocking collectives, per_device(): lax.psum(contract_rows(panel_rows, start_rows, None), ('row', 'depth'))  89.5 us
    psum x4, blocking collectives, find_zone_for(): r2 = psum(psum(target, device_axis), mesh_ax)  37.5 us
    psum x1, waiting for transfers between devices, per_device(): lax.psum(jnp.dot(panel_rows, mixed_cols, preferred_element_type=jnp.float...  36.9 us
    dot_general x5, matrix products, contract_rows(): lax.dot_general(left_side, right_side, (((0,), (0,)), ((), ())), precisio...  36.5 us
    dot_general x1, matrix products, per_device(): jnp.dot(panel_rows, mixed_cols, preferred_element_type=jnp.float32)  22.6 us
    dot_general x2, matrix products, orthonormal_pass(): jnp.dot(stored_basis, projection, precision=HIGHEST, preferred_element_ty...  17.2 us
    another operation x6, other arithmetic, factor_gram(): lower_factor = jnp.linalg.cholesky(gram_matrix)  13 us
  transfers between devices with their start and end apart: 5, of which 5 were waited for; matrix products, arithmetic and copies ran while one was open for 0% of the time, Pallas kernels for 0%

profile of v1, /device:TPU:0, one launch (start us, length us, event | category | flops | bytes accessed | tf_op | source)
XLA Modules:
  0.0 422.5 jit_solution(11012168473042099243)
XLA Ops:
  7.2 0.0 all-reduce.7.cloned.1.call-start
  7.2 2.4 all_gather.3
  9.6 20.5 %fusion.2 = f32[16384,64]{0,1:T(8,128)} fusion(bf16[3072,16384]{1,0:T(8,128)(2,1)} %param.6, s32[]{:T(128)S(6)} %select_n.11, bf16[3072,64]{0,1:T(8,128)(2,1)S(1)} %all_gather.3), kind=kOutput, calls=%fused_computation.2 | convolution fusion | flops 3221225472 | bytes 54723584 | tf_op jit(solution)/shard_map/dot_general | solution.py:20
  30.1 89.5 %all-reduce.16 = bf16[16384,64]{0,1:T(8,128)(2,1)S(1)} all-reduce(f32[16384,64]{0,1:T(8,128)} %fusion.2), channel_id=1, replica_groups=mesh['row'=4,'col'=4,'depth'=2] {'row','depth'}, use_global_device_ids=true, to_apply=%region_0.0 | all-reduce | flops 1048576 | bytes 6291456 | tf_op jit(solution)/shard_map/psum | solution.py:56
  119.6 22.6 %fusion = f32[1536,64]{0,1:T(8,128)} fusion(bf16[3072,16384]{1,0:T(8,128)(2,1)} %param.6, s32[]{:T(128)S(6)} %select_n.11, bf16[16384,64]{0,1:T(8,128)(2,1)S(1)} %all-reduce.16), kind=kOutput, calls=%fused_computation | convolution fusion | flops 3221225472 | bytes 52822020 | tf_op jit(solution)/shard_map/dot_general | solution.py:60
  142.2 0.0 all-reduce.7.cloned.1.call-update
  142.2 0.0 all-reduce.9.cloned.1.call-start
  142.3 36.9 %all-reduce.7.cloned.1.call-done = f32[1536,64]{0,1:T(8,128)} async-done(((f32[1536,64]{0,1:T(8,128)}), f32[1536,64]{0,1:T(8,128)}) %all-reduce.7.cloned.1.call-update) | async-done | bytes 393232 | tf_op jit(solution)/shard_map/psum | solution.py:59
  179.2 7.6 %fusion.10 = f32[1024,64]{0,1:T(8,128)} fusion(f32[1536,64]{0,1:T(8,128)} %all-reduce.7.cloned.1.call-done, f32[3072,1024]{1,0:T(8,128)} %param.8, s32[]{:T(128)S(6)} %select_n.11), kind=kOutput, calls=%fused_computation.10 | convolution fusion | flops 1207959552 | bytes 6946820 | tf_op jit(solution)/shard_map/dot_general | solution.py:20
  186.8 0.0 all-reduce.9.cloned.1.call-update
  186.8 0.0 all-reduce.11.cloned.1.call-start
  186.8 18.0 %all-reduce.9.cloned.1.call-done = f32[1024,64]{0,1:T(8,128)} async-done(((f32[1024,64]{0,1:T(8,128)}), f32[1024,64]{0,1:T(8,128)}) %all-reduce.9.cloned.1.call-update) | async-done | bytes 262160 | tf_op jit(solution)/shard_map/psum | solution.py:12
  204.8 0.0 all-reduce.11.cloned.1.call-update
  204.8 0.2 all-reduce.13.cloned.1.call-start
  205.1 46.8 %all-reduce.11.cloned.1.call-done = f32[1024,64]{0,1:T(8,128)} async-done(((f32[1024,64]{0,1:T(8,128)}), f32[1024,64]{0,1:T(8,128)}) %all-reduce.11.cloned.1.call-update) | async-done | bytes 262160 | tf_op jit(solution)/shard_map/psum | solution.py:12
  251.9 0.0 copy-start
  251.9 9.1 %fusion.12 = f32[1536,64]{0,1:T(8,128)S(1)} fusion(f32[1536,64]{0,1:T(8,128)} %all-reduce.7.cloned.1.call-done, f32[3072,1024]{1,0:T(8,128)} %param.8, s32[]{:T(128)S(6)} %select_n.11, f32[1024,64]{0,1:T(8,128)} %all-reduce.11.cloned.1.call-done), kind=kOutput, calls=%fused_computation.12 | convolution fusion | flops 1208123392 | bytes 7340036 | tf_op jit(solution)/shard_map/dot_general | solution.py:38
  261.0 0.5 fusion.56
  261.4 3.4 psum.74
  264.9 15.3 %psum.75 = f32[64,64]{0,1:T(8,128)S(1)} all-reduce(f32[64,64]{0,1:T(8,128)S(1)} %psum.74), channel_id=1, replica_groups=mesh['row'=4,'col'=4,'depth'=2] {'row'}, use_global_device_ids=true, to_apply=%region_5.0 | all-reduce | flops 4096 | bytes 32768 | tf_op jit(solution)/shard_map/psum | solution.py:12
  280.2 0.1 copy.12
  280.3 5.8 %cholesky.44 = f32[64,64]{1,0:T(8,128)S(1)} custom-call(f32[64,64]{1,0:T(8,128)S(1)} %fusion.32), custom_call_target="Cholesky" | custom-call | tf_op jit(solution)/shard_map/jit(cholesky)/cholesky | solution.py:30
  286.2 0.6 compare_reduce_fusion.1
  286.8 0.7 select_bitcast_fusion.1
  287.5 4.9 %custom-call.6 = f32[1,64,64]{1,2,0:T(8,128)S(1)} custom-call(f32[1,64,64]{2,1,0:T(8,128)S(1)} %select_bitcast_fusion.1), custom_call_target="InvertDiagBlocksLowerTriangular" | custom-call | tf_op jit(solution)/shard_map/jit(_solve_triangular)/triangular_solve | solution.py:32
  292.4 0.3 fusion.27
  292.7 0.5 fusion.57
  293.2 7.6 %fusion.6 = f32[1024,64]{0,1:T(8,128)} fusion(f32[1536,64]{0,1:T(8,128)S(1)} %fusion.57, f32[3072,1024]{1,0:T(8,128)} %param.8, s32[]{:T(128)S(6)} %select_n.11), kind=kOutput, calls=%fused_computation.6 | convolution fusion | flops 1207959552 | bytes 6946820 | tf_op jit(solution)/shard_map/dot_general | solution.py:20
  300.7 0.0 all-reduce.13.cloned.1.call-update
  300.7 0.3 all-reduce.15.cloned.1.call-start
  301.0 18.1 %all-reduce.13.cloned.1.call-done = f32[1024,64]{0,1:T(8,128)} async-done(((f32[1024,64]{0,1:T(8,128)}), f32[1024,64]{0,1:T(8,128)}) %all-reduce.13.cloned.1.call-update) | async-done | bytes 262160 | tf_op jit(solution)/shard_map/psum | solution.py:12
  319.1 0.0 all-reduce.15.cloned.1.call-update
  319.1 0.0 copy-done
  319.2 46.8 %all-reduce.15.cloned.1.call-done = f32[1024,64]{0,1:T(8,128)} async-done(((f32[1024,64]{0,1:T(8,128)}), f32[1024,64]{0,1:T(8,128)}) %all-reduce.15.cloned.1.call-update) | async-done | bytes 262160 | tf_op jit(solution)/shard_map/psum | solution.py:12
  366.0 8.1 %fusion.15 = f32[1536,64]{0,1:T(8,128)S(1)} fusion(f32[1536,64]{0,1:T(8,128)S(1)} %fusion.57, f32[3072,1024]{1,0:T(8,128)} %param.8, s32[]{:T(128)S(6)} %select_n.11, f32[1024,64]{0,1:T(8,128)} %all-reduce.15.cloned.1.call-done), kind=kOutput, calls=%fused_computation.13 | convolution fusion | flops 1208123392 | bytes 7340036 | tf_op jit(solution)/shard_map/dot_general | solution.py:38
  374.1 0.5 fusion.58
  374.6 3.4 psum.78
  378.0 15.4 %psum.79 = f32[64,64]{0,1:T(8,128)S(1)} all-reduce(f32[64,64]{0,1:T(8,128)S(1)} %psum.78), channel_id=1, replica_groups=mesh['row'=4,'col'=4,'depth'=2] {'row'}, use_global_device_ids=true, to_apply=%region_11.14 | all-reduce | flops 4096 | bytes 32768 | tf_op jit(solution)/shard_map/psum | solution.py:12
  393.4 0.1 copy.14
  393.5 5.8 %cholesky.55 = f32[64,64]{1,0:T(8,128)S(1)} custom-call(f32[64,64]{1,0:T(8,128)S(1)} %fusion.30), custom_call_target="Cholesky" | custom-call | tf_op jit(solution)/shard_map/jit(cholesky)/cholesky | solution.py:30
  399.4 0.6 compare_reduce_fusion
  400.0 2.1 fusion.34
  402.1 0.7 select_bitcast_fusion
  402.8 4.9 %custom-call.7 = f32[1,64,64]{1,2,0:T(8,128)S(1)} custom-call(f32[1,64,64]{2,1,0:T(8,128)S(1)} %select_bitcast_fusion), custom_call_target="InvertDiagBlocksLowerTriangular" | custom-call | tf_op jit(solution)/shard_map/jit(_solve_triangular)/triangular_solve | solution.py:32
  407.7 0.3 fusion.25
  408.0 0.5 fusion.59
  408.5 4.0 all_to_all.19
  412.5 0.8 copy.18
  413.3 2.0 fusion.19
  415.3 0.7 dynamic-slice_add_fusion
  (7 shorter events, 0.1 us)
Async XLA Ops:
  7.2 172.0 %all-reduce.7.cloned.1.call-start = ((), (), s32[]{:S(2)}) async-start(), calls=%async_computation.1 | async-start | bytes 786432 | tf_op jit(solution)/shard_map/psum | solution.py:59
  142.2 62.6 %all-reduce.9.cloned.1.call-start = ((), (), s32[]{:S(2)}) async-start(), calls=%async_computation.2 | async-start | bytes 524288 | tf_op jit(solution)/shard_map/psum | solution.py:12
  186.8 65.1 %all-reduce.11.cloned.1.call-start = ((), (), s32[]{:S(2)}) async-start(), calls=%async_computation.3 | async-start | bytes 524288 | tf_op jit(solution)/shard_map/psum | solution.py:12
  204.8 114.3 %all-reduce.13.cloned.1.call-start = ((), (), s32[]{:S(2)}) async-start(), calls=%async_computation.4 | async-start | bytes 524288 | tf_op jit(solution)/shard_map/psum | solution.py:12
  251.9 67.3 %copy-start = (f32[1024,64]{0,1:T(8,128)S(1)}, f32[1024,64]{0,1:T(8,128)}, u32[]{:S(2)}) copy-start(f32[1024,64]{0,1:T(8,128)} %all-reduce.11.cloned.1.call-done) | copy-start | bytes 786436
  300.7 65.3 %all-reduce.15.cloned.1.call-start = ((), (), s32[]{:S(2)}) async-start(), calls=%async_computation.5 | async-start | bytes 524288 | tf_op jit(solution)/shard_map/psum | solution.py:12
Sparse Core Ops, SparseCore 0:
  142.3 36.8 all-reduce.6
  186.9 17.8 all-reduce.8
  207.7 44.1 all-reduce.10
  300.9 18.2 all-reduce.12
  321.9 44.1 all-reduce.14
